TPU v7x, 32 devices: a whole 2x2x4 slice. The times are simulated.
32 devices in a mesh: req: 16 (over z, y, x), mlp: 2 (over core).
Axes of the slice: x: 2, y: 2, z: 4, core: 2. Of those that a mesh axis runs over, the one named last changes fastest.
Arguments:
- queries: bfloat16 [16, 256, 1536], P('req'), may hold values from -90 to 90
- cached_key_slots: bfloat16 [16, 8192, 512], P('req', 'mlp'), may hold values from -5 to 5
- cached_value_slots: bfloat16 [16, 8192, 512], P('req', 'mlp'), may hold values from -6 to 6
- new_token_keys: bfloat16 [16, 256, 512], P('req', 'mlp'), may hold values from -5.05 to 5.05
- new_token_values: bfloat16 [16, 256, 512], P('req', 'mlp'), may hold values from -6 to 6
- cache_len: int32 [16], replicated, may hold values from 1 to 8192, 65536 in all
- placing: int32 [16], replicated, may hold values from 0 to 15, each once
- w_gate: bfloat16 [1536, 12288], P('req', 'mlp'), may hold values from -0.15625 to 0.15625
- w_up: bfloat16 [1536, 12288], P('req', 'mlp'), may hold values from -0.15625 to 0.15625
- w_down: bfloat16 [12288, 1536], P('mlp', 'req'), may hold values from -0.0546875 to 0.0546875
Outputs:
- mixed: bfloat16 [16, 256, 1536], P('req', 'mlp')
All inputs are finite; a program needn't handle non-finite values.
Results may differ from a plain program's by a relative error of at most 0.019.
Values may be sent and summed in bfloat16 or wider, within the bound.
A program may use at most 192 MiB of HBM per device.

v0:
```python
import jax
import jax.numpy as jnp
from jax import lax
from jax.sharding import PartitionSpec as P

HEAD_SIZE = 256
QUERY_HEADS = 6
KEY_VALUE_HEADS = 2
score_scale = 0.0625
negative = -1e30


def lookup(table, index):
    positions = jnp.arange(table.shape[0], dtype=jnp.int32)
    return jnp.sum(jnp.where(positions == index, table, 0))


def rms_rows(attended):
    wide = attended.astype(jnp.float32)
    return (wide * lax.rsqrt(jnp.mean(wide * wide, axis=-1, keepdims=True) + 1e-06)).astype(
        jnp.bfloat16
    )


def gathered_weights(weighted, denom_local, w_gate, w_up, w_down):
    token_inputs = weighted.shape[0]
    mlp_index = lax.axis_index("mlp")
    row_count = token_inputs // lax.axis_size("mlp")
    weighted, denom = lax.psum((weighted, denom_local), "mlp")
    attended = (
        (weighted / jnp.transpose(denom, (2, 0, 1))[..., None])
        .reshape(token_inputs, QUERY_HEADS * HEAD_SIZE)
        .astype(jnp.bfloat16)
    )
    normed = rms_rows(attended)
    own_attended = lax.dynamic_slice_in_dim(attended, mlp_index * row_count, row_count, 0)
    gate_sum = jnp.dot(
        normed,
        lax.all_gather(w_gate, "req", axis=0, tiled=True),
        preferred_element_type=jnp.float32,
    )
    upper_sum = jnp.dot(
        normed, lax.all_gather(w_up, "req", axis=0, tiled=True), preferred_element_type=jnp.float32
    )
    hidden = (jax.nn.silu(gate_sum) * upper_sum).astype(jnp.bfloat16)
    partial_down = jnp.dot(
        hidden,
        lax.all_gather(w_down, "req", axis=1, tiled=True),
        preferred_element_type=jnp.float32,
    )
    own_rows = lax.psum_scatter(
        partial_down.astype(jnp.bfloat16), "mlp", scatter_dimension=0, tiled=True
    ).astype(jnp.float32)
    residual = own_attended.astype(jnp.float32)
    return (residual + own_rows).astype(jnp.bfloat16)[None]


def body(
    queries,
    cached_key_slots,
    cached_value_slots,
    new_token_keys,
    new_token_values,
    cache_len,
    placing,
    w_gate,
    w_up,
    w_down,
):
    slot_index = lax.axis_index("req")
    mlp_index = lax.axis_index("mlp")
    mlp_count = lax.axis_size("mlp")
    token_inputs = queries.shape[1]
    request_cache = cached_key_slots.shape[1]
    request_new_tokens = new_token_keys.shape[1]
    query_group_width = QUERY_HEADS // KEY_VALUE_HEADS
    row_count = token_inputs // mlp_count
    request = lookup(placing, slot_index)
    live_len = lookup(cache_len, request)
    query_head_rows = queries[0].reshape(
        token_inputs, KEY_VALUE_HEADS, query_group_width, HEAD_SIZE
    )
    request_keys = cached_key_slots[0].reshape(request_cache, KEY_VALUE_HEADS, HEAD_SIZE)
    request_values = cached_value_slots[0].reshape(request_cache, KEY_VALUE_HEADS, HEAD_SIZE)
    new_key_rows = new_token_keys[0].reshape(request_new_tokens, KEY_VALUE_HEADS, HEAD_SIZE)
    new_value_rows = new_token_values[0].reshape(request_new_tokens, KEY_VALUE_HEADS, HEAD_SIZE)
    cache_pos = mlp_index * request_cache + jnp.arange(request_cache, dtype=jnp.int32)
    cache_live = cache_pos < live_len
    scores_old = (
        jnp.einsum(
            "ngrd,cgd->grnc", query_head_rows, request_keys, preferred_element_type=jnp.float32
        )
        * score_scale
    )
    scores_old = jnp.where(cache_live[None, None, None, :], scores_old, negative)
    fresh_pos = mlp_index * request_new_tokens + jnp.arange(request_new_tokens, dtype=jnp.int32)
    causal = fresh_pos[None, :] <= jnp.arange(token_inputs, dtype=jnp.int32)[:, None]
    scores_new = (
        jnp.einsum(
            "ngrd,mgd->grnm", query_head_rows, new_key_rows, preferred_element_type=jnp.float32
        )
        * score_scale
    )
    scores_new = jnp.where(causal[None, None], scores_new, negative)
    local_top = jnp.maximum(scores_old.max(-1), scores_new.max(-1))
    row_top = lax.pmax(local_top, "mlp")
    expo_old = jnp.exp(scores_old - row_top[..., None])
    expo_new = jnp.exp(scores_new - row_top[..., None])
    denom_local = expo_old.sum(-1) + expo_new.sum(-1)
    probs_old = expo_old.astype(jnp.bfloat16)
    probs_new = expo_new.astype(jnp.bfloat16)
    weighted = jnp.einsum(
        "grnc,cgd->ngrd", probs_old, request_values, preferred_element_type=jnp.float32
    )
    weighted = weighted + jnp.einsum(
        "grnm,mgd->ngrd", probs_new, new_value_rows, preferred_element_type=jnp.float32
    )
    if lax.axis_size("req") > 16:
        return gathered_weights(weighted, denom_local, w_gate, w_up, w_down)
    w_in = jnp.stack([w_gate, w_up])
    w_in = lax.all_to_all(w_in, "req", split_axis=2, concat_axis=1, tiled=True)
    w_in = lax.all_gather(w_in, "mlp", axis=2, tiled=True)
    w_out = lax.all_to_all(w_down, "req", split_axis=0, concat_axis=1, tiled=True)
    w_out = lax.all_gather(w_out, "mlp", axis=0, tiled=True)
    denom_rows = jnp.transpose(denom_local, (2, 0, 1))
    weighted = lax.psum_scatter(weighted, "mlp", scatter_dimension=0, tiled=True)
    denom = lax.psum_scatter(denom_rows, "mlp", scatter_dimension=0, tiled=True)
    attended = (
        (weighted / denom[..., None])
        .reshape(row_count, QUERY_HEADS * HEAD_SIZE)
        .astype(jnp.bfloat16)
    )
    normed = lax.all_gather(rms_rows(attended), "req", axis=0, tiled=True)
    gate_sum = jnp.dot(normed, w_in[0], preferred_element_type=jnp.float32)
    upper_sum = jnp.dot(normed, w_in[1], preferred_element_type=jnp.float32)
    hidden = (jax.nn.silu(gate_sum) * upper_sum).astype(jnp.bfloat16)
    partial_down = jnp.dot(hidden, w_out, preferred_element_type=jnp.float32)
    own_rows = lax.psum_scatter(
        partial_down.astype(jnp.bfloat16), "req", scatter_dimension=0, tiled=True
    ).astype(jnp.float32)
    return (attended.astype(jnp.float32) + own_rows).astype(jnp.bfloat16)[None]


def solution(mesh):
    in_specs = (
        P("req", None, None),
        P("req", "mlp", None),
        P("req", "mlp", None),
        P("req", "mlp", None),
        P("req", "mlp", None),
        P(),
        P(),
        P("req", "mlp"),
        P("req", "mlp"),
        P("mlp", "req"),
    )
    out_specs = P("req", "mlp", None)
    return jax.shard_map(body, mesh=mesh, in_specs=in_specs, out_specs=out_specs, check_vma=False)
```

profile of v0, /device:TPU:0, one launch (start us, length us, event | category | flops | bytes accessed | tf_op | source)
XLA Modules:
  0.0 450.4 jit_solution(2439042109606651874)
XLA Ops:
  6.5 1.4 copy.59
  8.0 6.9 %reshape_squeeze.15 = bf16[4096,2,256]{2,1,0:T(2,128)(2,1)} reshape(bf16[1,4096,512]{2,1,0:T(8,128)(2,1)} %param.11) | data formatting | bytes 8388608 | tf_op jit(solution)/shard_map/reshape;squeeze | solution.py:83
  15.1 0.6 fusion.20
  15.8 1.3 fusion.21
  17.0 0.6 add_compare_fusion
  17.6 12.0 %bitcast_reduce_fusion = (f32[2,3,256]{2,1,0:T(4,128)S(1)}, f32[2,4096,256,3]{2,1,3,0:T(8,128)}) fusion(pred[4096]{0:T(1024)(128)(4,1)S(1)} %add_compare_fusion, bf16[256,2,3,256]{0,3,2,1:T(8,128)(2,1)S(1)} %bitcast.63, bf16[4096,2,256,1]{2,1,0,3:T(2,128)(2,1)} %bitcast.61), kind=kOutput, calls=%fused_computation.1 | convolution fusion | flops 3240098304 | bytes 30156800 | tf_op jit(solution)/shard_map/ngrd,cgd->grnc/dot_general | solution.py:90
  29.6 0.3 fusion.25
  29.9 2.6 pmax.7
  32.5 11.5 %fusion.1 = f32[2,3,256]{2,1,0:T(4,128)S(1)} fusion(f32[2,4096,256,3]{2,1,3,0:T(8,128)} %get-tuple-element.8, f32[2,3,256]{2,1,0:T(4,128)S(1)} %pmax.7, pred[4096]{0:T(1024)(128)(4,1)S(1)} %add_compare_fusion), kind=kLoop, calls=%fused_computation.4 | loop fusion | flops 25164288 | bytes 25182208 | tf_op jit(solution)/shard_map/reduce_sum | solution.py:109
  44.0 0.1 fusion.12
  44.2 0.8 copy.94
  45.0 1.5 pad_maximum_fusion
  46.5 5.3 %copy.69 = bf16[2,96,6144]{1,0,2:T(2,128)(2,1)} copy(bf16[2,96,6144]{2,1,0:T(8,128)(2,1)S(1)} %pad_maximum_fusion) | data formatting | bytes 4718592 | tf_op jit(solution)/shard_map/stack | solution.py:120
  51.9 8.2 %all-to-all-start = ((bf16[2,96,6144]{1,0,2:T(2,128)(2,1)}), bf16[2,96,6144]{1,0,2:T(2,128)(2,1)S(1)}, u32[]{:S(2)}, u32[]{:S(2)}) async-start(bf16[2,96,6144]{1,0,2:T(2,128)(2,1)} %copy.69), calls=%async_computation.1 | async-start | bytes 6291456 | tf_op jit(solution)/shard_map/all_to_all | solution.py:121
  60.1 6.9 %reshape_squeeze.18 = bf16[4096,2,256]{2,1,0:T(2,128)(2,1)} reshape(bf16[1,4096,512]{2,1,0:T(8,128)(2,1)} %param.12) | data formatting | bytes 8388608 | tf_op jit(solution)/shard_map/reshape;squeeze | solution.py:84
  67.1 13.5 %fusion.3 = f32[2,3,256,256]{3,2,1,0:T(8,128)S(1)} fusion(f32[2,4096,256,3]{2,1,3,0:T(8,128)} %get-tuple-element.8, f32[2,3,256]{2,1,0:T(4,128)S(1)} %pmax.7, pred[4096]{0:T(1024)(128)(4,1)S(1)} %add_compare_fusion, bf16[4096,2,256,1]{2,1,0,3:T(2,128)(2,1)} %bitcast.62), kind=kOutput, calls=%fused_computation.6 | convolution fusion | flops 3246391296 | bytes 30943232 | tf_op jit(solution)/shard_map/grnc,cgd->ngrd/dot_general | solution.py:112
  80.6 1.6 add_bitcast_fusion
  82.3 38.9 %all-to-all-done = bf16[2,96,6144]{1,0,2:T(2,128)(2,1)S(1)} async-done(((bf16[2,96,6144]{1,0,2:T(2,128)(2,1)}), bf16[2,96,6144]{1,0,2:T(2,128)(2,1)S(1)}, u32[]{:S(2)}, u32[]{:S(2)}) %all-to-all-start) | async-done | bytes 2359328 | tf_op jit(solution)/shard_map/all_to_all | solution.py:121
  121.2 5.5 %copy.91 = bf16[2,96,16,384]{3,1,2,0:T(8,128)(2,1)} copy(bf16[2,96,16,384]{1,0,3,2:T(2,128)(2,1)S(1)} %bitcast.56) | data formatting | bytes 4718592 | tf_op jit(solution)/shard_map/all_to_all | solution.py:121
  126.8 1.0 reshape.52
  128.0 1.4 multiply_reduce_fusion
  129.4 0.3 copy.68
  129.7 0.8 multiply_convert_fusion.1
  130.7 44.9 %all_to_all.37 = bf16[16,384,96]{1,2,0:T(8,128)(2,1)} all-to-all(bf16[16,384,96]{1,2,0:T(8,128)(2,1)S(1)} %bitcast.60), channel_id=1, replica_groups=mesh['req'=16,'mlp'=2] {'req'}, dimensions={0} | all-to-all | bytes 2359296 | tf_op jit(solution)/shard_map/all_to_all | solution.py:123
  175.6 0.2 reduce-scatter.8.cloned.1.call-start
  175.9 96.7 %all-gather.4.cloned.1.call-done = bf16[2048,1536]{0,1:T(8,128)(2,1)} async-done(((bf16[128,1536]{0,1:T(8,128)(2,1)}), bf16[2048,1536]{0,1:T(8,128)(2,1)}) %all-gather.4.cloned.1.call-update) | async-done | bytes 6291472 | tf_op jit(solution)/shard_map/all_gather | solution.py:133
  272.6 8.3 %fusion.9 = f32[2048,768]{1,0:T(8,128)S(1)} fusion(bf16[2048,1536]{0,1:T(8,128)(2,1)} %all-gather.4.cloned.1.call-done, bf16[2,1536,768]{2,1,0:T(8,128)(2,1)} %all-gather.6.cloned.1.call-done), kind=kOutput, calls=%fused_computation.15 | convolution fusion | flops 4831838208 | bytes 14942208 | tf_op jit(solution)/shard_map/dot_general | solution.py:134
  280.9 7.6 %multiply_convert_fusion = bf16[2048,768]{1,0:T(8,128)(2,1)} fusion(f32[2048,768]{1,0:T(8,128)S(1)} %fusion.9, bf16[2048,1536]{0,1:T(8,128)(2,1)S(1)} %copy-done.6, bf16[2,1536,768]{2,1,0:T(8,128)(2,1)S(1)} %copy-done.7), kind=kOutput, calls=%fused_computation.9 | convolution fusion | flops 4841275392 | bytes 18087936 | tf_op jit(solution)/shard_map/dot_general | solution.py:135
  288.5 9.1 %convolution_convert_fusion = bf16[2048,1536]{1,0:T(8,128)(2,1)} fusion(bf16[2048,768]{1,0:T(8,128)(2,1)} %multiply_convert_fusion, bf16[768,1536]{0,1:T(8,128)(2,1)} %all-gather.8.cloned.1.call-done), kind=kOutput, calls=%fused_computation.8 | convolution fusion | flops 4834983936 | bytes 11796480 | tf_op jit(solution)/shard_map/dot_general | solution.py:137
  297.7 0.3 copy.73
  298.0 143.7 %reduce-scatter.8.cloned.1.call-done = bf16[128,1536]{1,0:T(8,128)(2,1)} async-done(((bf16[2048,1536]{1,0:T(8,128)(2,1)}), bf16[128,1536]{1,0:T(8,128)(2,1)}) %reduce-scatter.8.cloned.1.call-update) | async-done | bytes 393232 | tf_op jit(solution)/shard_map/reduce_scatter | solution.py:138
  441.7 1.8 fusion.16
  (45 shorter events, 0.7 us)
Async XLA Ops:
  6.5 120.3 %reduce-scatter.10.cloned.1.call-start = ((), (), s32[]{:S(2)}) async-start(), calls=%async_computation.10 | async-start | bytes 196608
  6.5 8.4 %copy-start.4 = (bf16[1,128,512]{2,1,0:T(8,128)(2,1)S(1)}, bf16[1,128,512]{2,1,0:T(8,128)(2,1)}, u32[]{:S(2)}) copy-start(bf16[1,128,512]{2,1,0:T(8,128)(2,1)} %param.13) | copy-start | bytes 393220
  8.0 7.1 %copy-start.8 = (s32[16]{0:T(128)S(1)}, s32[16]{0:T(128)}, u32[]{:S(2)}) copy-start(s32[16]{0:T(128)} %param.16) | copy-start | bytes 196
  8.0 7.8 %copy-start.9 = (s32[16]{0:T(128)S(1)}, s32[16]{0:T(128)}, u32[]{:S(2)}) copy-start(s32[16]{0:T(128)} %param.15) | copy-start | bytes 196
  29.8 14.2 %copy-start = (f32[2,3,256,128]{2,3,1,0:T(8,128)}, f32[2,3,256,128]{2,3,1,0:T(8,128)S(1)}, u32[]{:S(2)}) copy-start(f32[2,3,256,128]{2,3,1,0:T(8,128)S(1)} %get-tuple-element.10) | copy-start | bytes 2359300
  32.5 12.5 %copy-start.3 = (bf16[96,6144]{1,0:T(8,128)(2,1)S(1)}, bf16[96,6144]{1,0:T(8,128)(2,1)}, u32[]{:S(2)}) copy-start(bf16[96,6144]{1,0:T(8,128)(2,1)} %param.18) | copy-start | bytes 3538948
  51.9 69.4 %all-to-all-start = ((bf16[2,96,6144]{1,0,2:T(2,128)(2,1)}), bf16[2,96,6144]{1,0,2:T(2,128)(2,1)S(1)}, u32[]{:S(2)}, u32[]{:S(2)}) async-start(bf16[2,96,6144]{1,0,2:T(2,128)(2,1)} %copy.69), calls=%async_computation.1 | async-start | bytes 6291456 | tf_op jit(solution)/shard_map/all_to_all | solution.py:121
  60.1 7.0 %copy-start.5 = (bf16[1,128,512]{2,1,0:T(8,128)(2,1)S(1)}, bf16[1,128,512]{2,1,0:T(8,128)(2,1)}, u32[]{:S(2)}) copy-start(bf16[1,128,512]{2,1,0:T(8,128)(2,1)} %param.14) | copy-start | bytes 393220
  60.1 67.9 %reduce-scatter.6.cloned.1.call-start = ((), (), s32[]{:S(2)}) async-start(), calls=%async_computation.5 | async-start | bytes 2359296 | tf_op jit(solution)/shard_map/reduce_scatter | solution.py:126
  67.1 13.5 %copy-start.1 = (f32[2,3,256,128]{2,3,1,0:T(8,128)S(1)}, f32[2,3,256,128]{2,3,1,0:T(8,128)}, u32[]{:S(2)}) copy-start(f32[2,3,256,128]{2,3,1,0:T(8,128)} %copy-done) | copy-start | bytes 2359300
  82.3 93.6 %all-gather.6.cloned.1.call-start = ((), (), s32[]{:S(2)}) async-start(), calls=%async_computation.7 | async-start | bytes 7077888 | tf_op jit(solution)/shard_map/all_gather | solution.py:122
  126.7 3.8 copy-start.2
  126.8 145.9 %all-gather.4.cloned.1.call-start = ((), (), s32[]{:S(2)}) async-start(), calls=%async_computation.6 | async-start | bytes 6684672 | tf_op jit(solution)/shard_map/all_gather | solution.py:133
  130.5 158.1 %all-gather.8.cloned.1.call-start = ((), (), s32[]{:S(2)}) async-start(), calls=%async_computation.8 | async-start | bytes 3538944 | tf_op jit(solution)/shard_map/all_gather | solution.py:124
  175.6 266.1 %reduce-scatter.8.cloned.1.call-start = ((), (), s32[]{:S(2)}) async-start(), calls=%async_computation.9 | async-start | bytes 6684672 | tf_op jit(solution)/shard_map/reduce_scatter | solution.py:138
  272.6 8.3 %copy-start.6 = (bf16[2048,1536]{0,1:T(8,128)(2,1)S(1)}, bf16[2048,1536]{0,1:T(8,128)(2,1)}, u32[]{:S(2)}) copy-start(bf16[2048,1536]{0,1:T(8,128)(2,1)} %all-gather.4.cloned.1.call-done) | copy-start | bytes 18874372
  272.6 8.3 %copy-start.7 = (bf16[2,1536,768]{2,1,0:T(8,128)(2,1)S(1)}, bf16[2,1536,768]{2,1,0:T(8,128)(2,1)}, u32[]{:S(2)}) copy-start(bf16[2,1536,768]{2,1,0:T(8,128)(2,1)} %all-gather.6.cloned.1.call-done) | copy-start | bytes 14155780
Sparse Core Ops, SparseCore 0:
  45.1 10.0 reduce-scatter.9
  82.4 10.3 reduce-scatter.5
  126.9 24.3 all-gather.5
  154.2 118.3 all-gather.3
  274.1 9.0 all-gather.7
  297.8 143.8 reduce-scatter.7
where the time goes:
time: 451 us; the launch traced here: 450 us
  waiting for transfers between devices  280 us (62%)
  matrix products  52.4 us (12%)
  blocking collectives  47.6 us (11%)
  local copies, waits for them, and re-layouts  28.9 us (6%)
  other arithmetic  19.7 us (4%)
  between operations  13.7 us (3%)
  starting transfers between devices  8.58 us (2%)
    reduce_scatter x1, waiting for transfers between devices, body(): lax.psum_scatter(partial_down.astype(jnp.bfloat16), 'req', scatter_dimens...  144 us
    all_gather x1, waiting for transfers between devices, body(): normed = lax.all_gather(rms_rows(attended), 'req', axis=0, tiled=True)  96.7 us
    all_to_all x1, blocking collectives, body(): lax.all_to_all(w_down, 'req', split_axis=0, concat_axis=1, tiled=True)  44.9 us
    all_to_all x1, waiting for transfers between devices, body(): w_in = lax.all_to_all(w_in, 'req', split_axis=2, concat_axis=1, tiled=True)  38.9 us
    dot_general x1, matrix products, body(): jnp.einsum('grnc,cgd->ngrd', probs_old, request_values, preferred_element...  13.5 us
    dot_general x1, matrix products, body(): jnp.einsum('ngrd,cgd->grnc', query_head_rows, request_keys, preferred_ele...  12 us
    reduce_sum x2, other arithmetic, body(): denom_local = expo_old.sum(-1) + expo_new.sum(-1)  11.7 us
    dot_general x1, matrix products, body(): partial_down = jnp.dot(hidden, w_out, preferred_element_type=jnp.float32)  9.13 us
  transfers between devices with their start and end apart: 7, of which 3 were waited for; matrix products, arithmetic and copies ran while one was open for 12% of the time, Pallas kernels for 0%

commit v1 on v0

--- a/solution.py
+++ b/solution.py
@@ -118,7 +118,9 @@
     if lax.axis_size("req") > 16:
         return gathered_weights(weighted, denom_local, w_gate, w_up, w_down)
     w_in = jnp.stack([w_gate, w_up])
-    w_in = lax.all_to_all(w_in, "req", split_axis=2, concat_axis=1, tiled=True)
+    cells = jnp.split(w_in, lax.axis_size("req"), axis=2)
+    incoming = lax.all_to_all(jnp.stack(cells), "req", 0, 0)
+    w_in = jnp.concatenate(incoming, axis=1)
     w_in = lax.all_gather(w_in, "mlp", axis=2, tiled=True)
     w_out = lax.all_to_all(w_down, "req", split_axis=0, concat_axis=1, tiled=True)
     w_out = lax.all_gather(w_out, "mlp", axis=0, tiled=True)

time: 451 us -> 434 us (0.962)
  waiting for transfers between devices: 280 us -> 266 us
  other arithmetic: 19.7 us -> 29.4 us
  local copies, waits for them, and re-layouts: 28.9 us -> 19.7 us
    all_to_all x1, waiting for transfers between devices: 38.9 us -> 25.5 us  [body(): incoming = lax.all_to_all(jnp.stack(cells), 'req', 0, 0)]
    unnamed x0 -> x15, other arithmetic: none -> 10.1 us
    another operation x1 -> x0, local copies, waits for them, and re-layouts: 5.33 us -> none  [body(): w_in = jnp.stack([w_gate, w_up])]
  transfers between devices with their start and end apart: 7 -> 7, of which waited for: 3 -> 3; matrix products, arithmetic and copies ran while one was open for 12% -> 13% of each run, Pallas kernels for 0% -> 0%
where the time goes in v1:
time: 434 us; the launch traced here: 433 us
  waiting for transfers between devices  266 us (61%)
  matrix products  52.3 us (12%)
  blocking collectives  43.4 us (10%)
  other arithmetic  29.4 us (7%)
  local copies, waits for them, and re-layouts  19.7 us (5%)
  between operations  13.7 us (3%)
  starting transfers between devices  8.59 us (2%)
    reduce_scatter x1, waiting for transfers between devices, body(): lax.psum_scatter(partial_down.astype(jnp.bfloat16), 'req', scatter_dimens...  144 us
    all_gather x1, waiting for transfers between devices, body(): normed = lax.all_gather(rms_rows(attended), 'req', axis=0, tiled=True)  96.8 us
    all_to_all x1, blocking collectives, body(): lax.all_to_all(w_down, 'req', split_axis=0, concat_axis=1, tiled=True)  40.8 us
    all_to_all x1, waiting for transfers between devices, body(): incoming = lax.all_to_all(jnp.stack(cells), 'req', 0, 0)  25.5 us
    dot_general x1, matrix products, body(): jnp.einsum('grnc,cgd->ngrd', probs_old, request_values, preferred_element...  13.5 us
    dot_general x1, matrix products, body(): jnp.einsum('ngrd,cgd->grnc', query_head_rows, request_keys, preferred_ele...  12 us
    reduce_sum x2, other arithmetic, body(): denom_local = expo_old.sum(-1) + expo_new.sum(-1)  11.7 us
    unnamed x15, other arithmetic  10.1 us
  transfers between devices with their start and end apart: 7, of which 3 were waited for; matrix products, arithmetic and copies ran while one was open for 13% of the time, Pallas kernels for 0%

profile of v1, /device:TPU:0, one launch (start us, length us, event | category | flops | bytes accessed | tf_op | source)
XLA Modules:
  0.0 433.4 jit_solution(8052339502175823979)
XLA Ops:
  6.5 1.4 copy.72
  8.0 7.0 %reshape_squeeze.15 = bf16[4096,2,256]{2,1,0:T(2,128)(2,1)} reshape(bf16[1,4096,512]{2,1,0:T(8,128)(2,1)} %param.11) | data formatting | bytes 8388608 | tf_op jit(solution)/shard_map/reshape;squeeze | solution.py:83
  15.8 1.4 fusion.38
  17.1 0.7 add_compare_fusion
  17.8 12.0 %bitcast_reduce_fusion = (f32[2,3,256]{2,1,0:T(4,128)S(1)}, f32[2,4096,256,3]{2,1,3,0:T(8,128)}) fusion(pred[4096]{0:T(1024)(128)(4,1)S(1)} %add_compare_fusion, bf16[256,2,3,256]{0,3,2,1:T(8,128)(2,1)S(1)} %bitcast.126, bf16[4096,2,256,1]{2,1,0,3:T(2,128)(2,1)} %bitcast.124), kind=kOutput, calls=%fused_computation.1 | convolution fusion | flops 3240098304 | bytes 30156800 | tf_op jit(solution)/shard_map/ngrd,cgd->grnc/dot_general | solution.py:90
  30.1 2.6 pmax.7
  32.7 11.6 %fusion.1 = f32[2,3,256]{2,1,0:T(4,128)S(1)} fusion(f32[2,4096,256,3]{2,1,3,0:T(8,128)} %get-tuple-element.8, f32[2,3,256]{2,1,0:T(4,128)S(1)} %pmax.7, pred[4096]{0:T(1024)(128)(4,1)S(1)} %add_compare_fusion), kind=kLoop, calls=%fused_computation.4 | loop fusion | flops 25164288 | bytes 25182208 | tf_op jit(solution)/shard_map/reduce_sum | solution.py:109
  44.5 0.8 copy.103
  45.3 0.7 bitcast_dynamic-update-slice_fusion.14
  47.3 0.7 bitcast_dynamic-update-slice_fusion.11
  48.7 0.7 bitcast_dynamic-update-slice_fusion.9
  49.4 0.7 bitcast_dynamic-update-slice_fusion.8
  50.1 0.7 bitcast_dynamic-update-slice_fusion.7
  50.7 0.7 bitcast_dynamic-update-slice_fusion.6
  54.1 0.7 bitcast_dynamic-update-slice_fusion.1
  55.4 0.7 fusion.34
  56.1 8.2 %all-to-all-start = ((bf16[16,2,96,384]{3,2,1,0:T(8,128)(2,1)}), bf16[16,2,96,384]{3,2,1,0:T(8,128)(2,1)S(1)}, u32[]{:S(2)}, u32[]{:S(2)}) async-start(bf16[16,2,96,384]{3,2,1,0:T(8,128)(2,1)} %fusion.34), calls=%async_computation.1 | async-start | bytes 4718592 | tf_op jit(solution)/shard_map/all_to_all | solution.py:122
  64.4 6.9 %reshape_squeeze.18 = bf16[4096,2,256]{2,1,0:T(2,128)(2,1)} reshape(bf16[1,4096,512]{2,1,0:T(8,128)(2,1)} %param.12) | data formatting | bytes 8388608 | tf_op jit(solution)/shard_map/reshape;squeeze | solution.py:84
  71.4 13.5 %fusion.3 = f32[2,3,256,256]{3,2,1,0:T(8,128)S(1)} fusion(f32[2,4096,256,3]{2,1,3,0:T(8,128)} %get-tuple-element.8, f32[2,3,256]{2,1,0:T(4,128)S(1)} %pmax.7, pred[4096]{0:T(1024)(128)(4,1)S(1)} %add_compare_fusion, bf16[4096,2,256,1]{2,1,0,3:T(2,128)(2,1)} %bitcast.125), kind=kOutput, calls=%fused_computation.6 | convolution fusion | flops 3246391296 | bytes 30943232 | tf_op jit(solution)/shard_map/grnc,cgd->ngrd/dot_general | solution.py:112
  84.8 1.6 add_bitcast_fusion
  86.5 25.5 %all-to-all-done = bf16[16,2,96,384]{3,2,1,0:T(8,128)(2,1)S(1)} async-done(((bf16[16,2,96,384]{3,2,1,0:T(8,128)(2,1)}), bf16[16,2,96,384]{3,2,1,0:T(8,128)(2,1)S(1)}, u32[]{:S(2)}, u32[]{:S(2)}) %all-to-all-start) | async-done | bytes 2359328 | tf_op jit(solution)/shard_map/all_to_all | solution.py:122
  112.0 1.7 copy.82
  113.8 1.0 reshape.60
  114.8 1.5 multiply_reduce_fusion
  116.6 0.8 multiply_convert_fusion.1
  117.6 40.8 %all_to_all.24 = bf16[16,384,96]{1,2,0:T(8,128)(2,1)} all-to-all(bf16[16,384,96]{1,2,0:T(8,128)(2,1)S(1)} %bitcast.123), channel_id=1, replica_groups=mesh['req'=16,'mlp'=2] {'req'}, dimensions={0} | all-to-all | bytes 2359296 | tf_op jit(solution)/shard_map/all_to_all | solution.py:125
  158.7 96.8 %all-gather.4.cloned.1.call-done = bf16[2048,1536]{0,1:T(8,128)(2,1)} async-done(((bf16[128,1536]{0,1:T(8,128)(2,1)}), bf16[2048,1536]{0,1:T(8,128)(2,1)}) %all-gather.4.cloned.1.call-update) | async-done | bytes 6291472 | tf_op jit(solution)/shard_map/all_gather | solution.py:135
  255.5 8.3 %fusion.9 = f32[2048,768]{1,0:T(8,128)S(1)} fusion(bf16[2048,1536]{0,1:T(8,128)(2,1)} %all-gather.4.cloned.1.call-done, bf16[2,1536,768]{2,1,0:T(8,128)(2,1)} %all-gather.6.cloned.1.call-done), kind=kOutput, calls=%fused_computation.45 | convolution fusion | flops 4831838208 | bytes 14942208 | tf_op jit(solution)/shard_map/dot_general | solution.py:136
  263.8 7.6 %multiply_convert_fusion = bf16[2048,768]{1,0:T(8,128)(2,1)} fusion(f32[2048,768]{1,0:T(8,128)S(1)} %fusion.9, bf16[2048,1536]{0,1:T(8,128)(2,1)S(1)} %copy-done.5, bf16[2,1536,768]{2,1,0:T(8,128)(2,1)S(1)} %copy-done.6), kind=kOutput, calls=%fused_computation.39 | convolution fusion | flops 4841275392 | bytes 18087936 | tf_op jit(solution)/shard_map/dot_general | solution.py:137
  271.4 9.1 %convolution_convert_fusion = bf16[2048,1536]{1,0:T(8,128)(2,1)} fusion(bf16[2048,768]{1,0:T(8,128)(2,1)} %multiply_convert_fusion, bf16[768,1536]{0,1:T(8,128)(2,1)} %all-gather.8.cloned.1.call-done), kind=kOutput, calls=%fused_computation.8 | convolution fusion | flops 4834983936 | bytes 11796480 | tf_op jit(solution)/shard_map/dot_general | solution.py:139
  280.8 143.9 %reduce-scatter.8.cloned.1.call-done = bf16[128,1536]{1,0:T(8,128)(2,1)} async-done(((bf16[2048,1536]{1,0:T(8,128)(2,1)}), bf16[128,1536]{1,0:T(8,128)(2,1)}) %reduce-scatter.8.cloned.1.call-update) | async-done | bytes 393232 | tf_op jit(solution)/shard_map/reduce_scatter | solution.py:140
  424.7 1.8 fusion.16
  (57 shorter events, 7.9 us)
Async XLA Ops:
  6.5 107.2 %reduce-scatter.10.cloned.1.call-start = ((), (), s32[]{:S(2)}) async-start(), calls=%async_computation.10 | async-start | bytes 196608
  7.9 7.0 %copy-start.3 = (bf16[1,128,512]{2,1,0:T(8,128)(2,1)S(1)}, bf16[1,128,512]{2,1,0:T(8,128)(2,1)}, u32[]{:S(2)}) copy-start(bf16[1,128,512]{2,1,0:T(8,128)(2,1)} %param.13) | copy-start | bytes 393220
  8.0 7.2 %copy-start.7 = (s32[16]{0:T(128)S(1)}, s32[16]{0:T(128)}, u32[]{:S(2)}) copy-start(s32[16]{0:T(128)} %param.16) | copy-start | bytes 196
  8.0 7.8 %copy-start.8 = (s32[16]{0:T(128)S(1)}, s32[16]{0:T(128)}, u32[]{:S(2)}) copy-start(s32[16]{0:T(128)} %param.15) | copy-start | bytes 196
  32.7 12.6 %copy-start = (bf16[96,6144]{1,0:T(8,128)(2,1)S(1)}, bf16[96,6144]{1,0:T(8,128)(2,1)}, u32[]{:S(2)}) copy-start(bf16[96,6144]{1,0:T(8,128)(2,1)} %param.18) | copy-start | bytes 3538948
  32.7 12.6 %copy-start.1 = (bf16[96,6144]{1,0:T(8,128)(2,1)S(1)}, bf16[96,6144]{1,0:T(8,128)(2,1)}, u32[]{:S(2)}) copy-start(bf16[96,6144]{1,0:T(8,128)(2,1)} %param.17) | copy-start | bytes 3538948
  56.1 55.8 %all-to-all-start = ((bf16[16,2,96,384]{3,2,1,0:T(8,128)(2,1)}), bf16[16,2,96,384]{3,2,1,0:T(8,128)(2,1)S(1)}, u32[]{:S(2)}, u32[]{:S(2)}) async-start(bf16[16,2,96,384]{3,2,1,0:T(8,128)(2,1)} %fusion.34), calls=%async_computation.1 | async-start | bytes 4718592 | tf_op jit(solution)/shard_map/all_to_all | solution.py:122
  64.3 7.0 %copy-start.4 = (bf16[1,128,512]{2,1,0:T(8,128)(2,1)S(1)}, bf16[1,128,512]{2,1,0:T(8,128)(2,1)}, u32[]{:S(2)}) copy-start(bf16[1,128,512]{2,1,0:T(8,128)(2,1)} %param.14) | copy-start | bytes 393220
  64.3 50.5 %reduce-scatter.6.cloned.1.call-start = ((), (), s32[]{:S(2)}) async-start(), calls=%async_computation.5 | async-start | bytes 2359296 | tf_op jit(solution)/shard_map/reduce_scatter | solution.py:128
  86.4 72.3 %all-gather.6.cloned.1.call-start = ((), (), s32[]{:S(2)}) async-start(), calls=%async_computation.7 | async-start | bytes 7077888 | tf_op jit(solution)/shard_map/all_gather | solution.py:124
  113.7 141.7 %all-gather.4.cloned.1.call-start = ((), (), s32[]{:S(2)}) async-start(), calls=%async_computation.6 | async-start | bytes 6684672 | tf_op jit(solution)/shard_map/all_gather | solution.py:135
  114.8 2.7 copy-start.2
  117.5 153.9 %all-gather.8.cloned.1.call-start = ((), (), s32[]{:S(2)}) async-start(), calls=%async_computation.8 | async-start | bytes 3538944 | tf_op jit(solution)/shard_map/all_gather | solution.py:126
  158.4 266.3 %reduce-scatter.8.cloned.1.call-start = ((), (), s32[]{:S(2)}) async-start(), calls=%async_computation.9 | async-start | bytes 6684672 | tf_op jit(solution)/shard_map/reduce_scatter | solution.py:140
  255.5 8.3 %copy-start.5 = (bf16[2048,1536]{0,1:T(8,128)(2,1)S(1)}, bf16[2048,1536]{0,1:T(8,128)(2,1)}, u32[]{:S(2)}) copy-start(bf16[2048,1536]{0,1:T(8,128)(2,1)} %all-gather.4.cloned.1.call-done) | copy-start | bytes 18874372
  255.5 8.3 %copy-start.6 = (bf16[2,1536,768]{2,1,0:T(8,128)(2,1)S(1)}, bf16[2,1536,768]{2,1,0:T(8,128)(2,1)}, u32[]{:S(2)}) copy-start(bf16[2,1536,768]{2,1,0:T(8,128)(2,1)} %all-gather.6.cloned.1.call-done) | copy-start | bytes 14155780
Sparse Core Ops, SparseCore 0:
  45.4 10.0 reduce-scatter.9
  86.6 10.3 reduce-scatter.5
  113.8 20.2 all-gather.5
  137.1 118.3 all-gather.3
  256.9 9.0 all-gather.7
  280.7 143.9 reduce-scatter.7
